TPU v7x, 128 devices: a whole 4x4x4 slice. The times are simulated.
128 devices in a mesh: section: 2 (over core), blk: 16 (over y, x), mp: 4 (over z).
Axes of the slice: x: 4, y: 4, z: 4, core: 2. Of those that a mesh axis runs over, the one named last changes fastest.
Arguments:
- patches: bfloat16 [256, 5120], P('section'), may hold values from -6 to 6
- merge_gain: float32 [1280], replicated, may hold values from 0.25 to 1.75
- merge_first: bfloat16 [5120, 5120], P(None, ('blk', 'mp')), may hold values from -0.078125 to 0.078125
- merge_second: bfloat16 [5120, 4096], P(('blk', 'mp')), may hold values from -0.078125 to 0.078125
- text_embeds: bfloat16 [4, 1024, 4096], P(None, 'blk', 'mp'), may hold values from -7 to 14
- positions: int32 [256], replicated, may hold values from 0 to 4095, as said below
- segments: int32 [4096], replicated, may hold values from 0 to 2, never falling along the last dimension, each value on 1 to 2048 neighbouring positions
- norm_gain: float32 [2, 4096], P('section'), may hold values from 0.25 to 1.75
- query_weight: bfloat16 [2, 4096, 4096], P('section', 'blk', 'mp'), may hold values from -1 to 1
- keyval_weight: bfloat16 [2, 4096, 4, 2, 128], P('section', 'blk', 'mp'), may hold values from -1 to 1
- out_weight: bfloat16 [2, 4096, 4096], P('section', 'mp', 'blk'), may hold values from -0.09375 to 0.09375
Outputs:
- hidden: bfloat16 [2, 4, 1024, 4096], P('section', None, 'blk', 'mp')
Inputs may be any that keep to these rules, and one draw needn't show every extreme that they name: `positions`: distinct and increasing.
All inputs are finite; a program needn't handle non-finite values.
Results may differ from a plain program's by a relative error of at most 0.015.
Values may be sent and summed in bfloat16 or wider, within the bound.
No kernel may reach another device: no remote copies, remote signals or barrier semaphores. Data moves between devices by JAX's collectives and lax.ppermute only.
A program may use at most 128 MiB of HBM per device.

v0:
```python
import jax
import jax.numpy as jnp
from jax import lax
from jax.sharding import PartitionSpec as P

epsilon = 1e-06
rope_base = 1000000.0


def shifted(value, axis, by):
    size = lax.axis_size(axis)
    pairs = [(i, i + by) for i in range(size) if 0 <= i + by < size]
    return lax.ppermute(value, axis, pairs)


def rope_tables(where_at, head_size):
    steps_half = jnp.arange(head_size // 2).astype(jnp.float32)
    inverse = jnp.exp(-jnp.log(rope_base) * 2.0 * steps_half / head_size)
    angles = where_at.astype(jnp.float32)[:, None] * inverse[None, :]
    return (jnp.cos(angles), jnp.sin(angles))


def rotate(values, cosine, sine):
    half = values.shape[-1] // 2
    first = values[..., :half]
    second = values[..., half:]
    cosine = cosine[:, None, :]
    sine = sine[:, None, :]
    return jnp.concatenate(
        [first * cosine - second * sine, second * cosine + first * sine], axis=-1
    )


def local(
    patches,
    merge_gain,
    merge_first,
    merge_second,
    text_embeds,
    positions,
    segments,
    norm_gain,
    query_weight,
    keyval_weight,
    out_weight,
):
    count = patches.shape[0]
    width = merge_gain.shape[0]
    blocks = text_embeds.shape[0]
    rows_here = text_embeds.shape[1]
    slice_width = text_embeds.shape[2]
    seq_len = segments.shape[0]
    block_len = seq_len // blocks
    section_index = lax.axis_index("section")
    cycle_index = lax.axis_index("blk")
    model_index = lax.axis_index("mp")
    pieces = patches.astype(jnp.float32).reshape(count, -1, width)
    centered = pieces - jnp.mean(pieces, axis=-1, keepdims=True)
    variance = jnp.mean(centered * centered, axis=-1, keepdims=True)
    normed = (
        (centered * lax.rsqrt(variance + epsilon) * merge_gain)
        .reshape(count, -1)
        .astype(jnp.bfloat16)
    )
    inner = jax.nn.gelu(
        jnp.dot(normed, merge_first, preferred_element_type=jnp.float32), approximate=False
    ).astype(jnp.bfloat16)
    partial_merge = jnp.dot(inner, merge_second, preferred_element_type=jnp.float32)
    merged_full = lax.psum(partial_merge, ("blk", "mp")).astype(jnp.bfloat16)
    merged_mine = lax.dynamic_slice_in_dim(merged_full, model_index * slice_width, slice_width, 1)
    visual_all = lax.all_gather(merged_mine, "section", axis=0, tiled=True)
    query_full, keyval_full, out_full = (
        lax.all_gather(query_weight, "blk", axis=1, tiled=True),
        lax.all_gather(keyval_weight, "blk", axis=1, tiled=True),
        lax.all_gather(out_weight, "blk", axis=2, tiled=True),
    )
    query_full = query_full[0]
    kv_heads = keyval_full.shape[2]
    head_size = keyval_full.shape[4]
    keyval_full = keyval_full[0].reshape(keyval_full.shape[1], -1)
    out_full = out_full[0]
    gain_here = norm_gain[0]
    group = query_full.shape[1] // (kv_heads * head_size)
    scale = 1.0 / head_size**0.5
    key_where = jnp.arange(seq_len)
    ticks = blocks + lax.axis_size("section") - 1
    zero_index = jnp.zeros((), jnp.int32)
    held = jnp.zeros((rows_here, slice_width), jnp.bfloat16)
    cache_keys = jnp.zeros((seq_len, kv_heads, head_size), jnp.bfloat16)
    cache_values = jnp.zeros((seq_len, kv_heads, head_size), jnp.bfloat16)
    outputs = jnp.zeros((blocks, rows_here, slice_width), jnp.bfloat16)
    for tick_now in range(ticks):
        bound = min(tick_now + 1, blocks) * block_len
        block_now = tick_now - section_index
        active = (block_now >= 0) & (block_now < blocks)
        block_safe = jnp.clip(block_now, 0, blocks - 1)
        row_where = block_safe * block_len + cycle_index * rows_here + jnp.arange(rows_here)
        is_visual = positions[None, :] == row_where[:, None]
        picked = jnp.dot(
            is_visual.astype(jnp.bfloat16), visual_all, preferred_element_type=jnp.float32
        ).astype(jnp.bfloat16)
        text_rows = lax.dynamic_index_in_dim(text_embeds, block_safe, 0, keepdims=False)
        embedded = jnp.where(jnp.any(is_visual, axis=1)[:, None], picked, text_rows)
        incoming = jnp.where(section_index == 0, embedded, held)
        features = lax.all_gather(incoming, "mp", axis=1, tiled=True)
        feat_f = features.astype(jnp.float32)
        normx = (
            feat_f
            * lax.rsqrt(jnp.mean(feat_f * feat_f, axis=-1, keepdims=True) + epsilon)
            * gain_here
        ).astype(jnp.bfloat16)
        cosine, sine = rope_tables(row_where, head_size)
        query = jnp.dot(normx, query_full, preferred_element_type=jnp.float32).reshape(
            rows_here, -1, head_size
        )
        query = (
            rotate(query, cosine, sine)
            .astype(jnp.bfloat16)
            .reshape(rows_here, kv_heads, group, head_size)
        )
        keyval = jnp.dot(normx, keyval_full, preferred_element_type=jnp.float32).reshape(
            rows_here, kv_heads, 2, head_size
        )
        new_keys = rotate(keyval[:, :, 0, :], cosine, sine).astype(jnp.bfloat16)
        new_values = keyval[:, :, 1, :].astype(jnp.bfloat16)
        block_keys, block_values = (
            lax.all_gather(new_keys, "blk", axis=0, tiled=True),
            lax.all_gather(new_values, "blk", axis=0, tiled=True),
        )
        start = block_safe * block_len
        cache_keys = jnp.where(
            active,
            lax.dynamic_update_slice(cache_keys, block_keys, (start, zero_index, zero_index)),
            cache_keys,
        )
        cache_values = jnp.where(
            active,
            lax.dynamic_update_slice(cache_values, block_values, (start, zero_index, zero_index)),
            cache_values,
        )
        keys_seen = cache_keys[:bound]
        values_seen = cache_values[:bound]
        scores = (
            jnp.einsum("qkgd,skd->kgqs", query, keys_seen, preferred_element_type=jnp.float32)
            * scale
        )
        row_segments = jnp.take(segments, row_where)
        allowed = (key_where[None, :bound] <= row_where[:, None]) & (
            segments[None, :bound] == row_segments[:, None]
        )
        scores = jnp.where(allowed[None, None], scores, -jnp.inf)
        top = jnp.max(scores, axis=-1, keepdims=True)
        expo = jnp.exp(scores - top)
        probs = (expo / jnp.sum(expo, axis=-1, keepdims=True)).astype(jnp.bfloat16)
        attended = jnp.einsum(
            "kgqs,skd->qkgd", probs, values_seen, preferred_element_type=jnp.float32
        )
        attended = attended.reshape(rows_here, -1).astype(jnp.bfloat16)
        term = jnp.dot(attended, out_full, preferred_element_type=jnp.float32)
        summed = lax.psum_scatter(
            term.astype(jnp.bfloat16), "mp", scatter_dimension=1, tiled=True
        ).astype(jnp.float32)
        result = (incoming.astype(jnp.float32) + summed).astype(jnp.bfloat16)
        outputs = jnp.where(
            active,
            lax.dynamic_update_slice(outputs, result[None], (block_safe, zero_index, zero_index)),
            outputs,
        )
        held = shifted(result, "section", 1)
    return outputs[None]


def solution(mesh):
    return jax.shard_map(
        local,
        mesh=mesh,
        in_specs=(
            P("section", None),
            P(),
            P(None, ("blk", "mp")),
            P(("blk", "mp"), None),
            P(None, "blk", "mp"),
            P(),
            P(),
            P("section", None),
            P("section", "blk", "mp"),
            P("section", "blk", "mp", None, None),
            P("section", "mp", "blk"),
        ),
        out_specs=P("section", None, "blk", "mp"),
        check_vma=False,
    )
```

profile of v0, /device:TPU:0, one launch (start us, length us, event | category | flops | bytes accessed | tf_op | source)
XLA Modules:
  0.0 948.9 jit_solution(6913599249277682439)
XLA Ops:
  8.8 2.9 reshape.1266
  14.3 1.9 copy.38
  16.2 5.2 fusion.210
  23.5 383.3 %all-reduce.1 = bf16[128,4096]{1,0:T(8,128)(2,1)S(1)} all-reduce(f32[128,4096]{1,0:T(8,128)} %fusion.210), channel_id=1, replica_groups=mesh['section'=2,'blk'=16,'mp'=4] {'blk','mp'}, use_global_device_ids=true, to_apply=%region_3.4 | all-reduce | flops 524288 | bytes 3145728 | tf_op jit(solution)/shard_map/psum | solution.py:69
  407.7 2.2 all_gather.57
  411.0 13.4 %all_gather.58 = bf16[64,4096]{1,0:T(8,128)(2,1)S(1)} all-gather(bf16[64,1024]{1,0:T(8,128)(2,1)S(1)} %fusion.63), channel_id=1, replica_groups=mesh['section'=2,'blk'=16,'mp'=4] {'mp'}, dimensions={1}, use_global_device_ids=true | all-gather | bytes 655360 | tf_op jit(solution)/shard_map/all_gather | solution.py:105
  424.8 1.3 multiply_cosine_fusion
  426.1 4.7 copy.37
  432.0 20.7 %all_gather.61 = bf16[1024,1,128]{2,0,1:T(8,128)(2,1)S(1)} all-gather(bf16[64,1,128]{2,0,1:T(8,128)(2,1)S(1)} %pad_maximum_fusion), channel_id=1, replica_groups=mesh['section'=2,'blk'=16,'mp'=4] {'blk'}, dimensions={0}, use_global_device_ids=true | all-gather | bytes 278528 | tf_op jit(solution)/shard_map/all_gather | solution.py:127
  452.7 24.1 %all-gather = bf16[1024,1,1,128]{3,0,2,1:T(8,128)(2,1)S(1)} all-gather(bf16[64,1,1,128]{3,0,2,1:T(8,128)(2,1)S(1)} %slice.285), channel_id=2, replica_groups=mesh['section'=2,'blk'=16,'mp'=4] {'blk'}, dimensions={0}, use_global_device_ids=true | all-gather | bytes 278528 | tf_op jit(solution)/shard_map/all_gather | solution.py:128
  480.5 11.8 %copy.31 = bf16[1024,4096]{1,0:T(8,128)(2,1)} copy(bf16[1024,4096]{0,1:T(8,128)(2,1)} %bitcast.333) | data formatting | bytes 16777216 | tf_op jit(solution)/shard_map/dot_general | solution.py:113
  492.3 6.1 fusion.125
  498.5 1.5 fusion.311
  500.6 1.5 fusion.72
  502.2 5.8 fusion.13
  511.2 15.4 %reduce-scatter.6.cloned.1.call-done = bf16[64,1024]{1,0:T(8,128)(2,1)} async-done(((bf16[64,4096]{1,0:T(8,128)(2,1)}), bf16[64,1024]{1,0:T(8,128)(2,1)}) %reduce-scatter.6.cloned.1.call-update) | async-done | bytes 131088 | tf_op jit(solution)/shard_map/reduce_scatter | solution.py:160
  527.7 1.3 collective-permute-start
  531.9 13.5 %all_gather.64 = bf16[64,4096]{1,0:T(8,128)(2,1)S(1)} all-gather(bf16[64,1024]{1,0:T(8,128)(2,1)S(1)} %fusion.65), channel_id=1, replica_groups=mesh['section'=2,'blk'=16,'mp'=4] {'mp'}, dimensions={1}, use_global_device_ids=true | all-gather | bytes 655360 | tf_op jit(solution)/shard_map/all_gather | solution.py:105
  546.5 6.1 fusion.128
  552.6 23.8 %all-gather.1 = bf16[1024,1,1,128]{3,0,2,1:T(8,128)(2,1)S(1)} all-gather(bf16[64,1,1,128]{3,0,2,1:T(8,128)(2,1)S(1)} %slice.284), channel_id=3, replica_groups=mesh['section'=2,'blk'=16,'mp'=4] {'blk'}, dimensions={0}, use_global_device_ids=true | all-gather | bytes 278528 | tf_op jit(solution)/shard_map/all_gather | solution.py:128
  576.7 23.3 %all_gather.66 = bf16[1024,1,128]{2,0,1:T(8,128)(2,1)S(1)} all-gather(bf16[64,1,128]{2,0,1:T(8,128)(2,1)S(1)} %pad_maximum_fusion.1), channel_id=1, replica_groups=mesh['section'=2,'blk'=16,'mp'=4] {'blk'}, dimensions={0}, use_global_device_ids=true | all-gather | bytes 278528 | tf_op jit(solution)/shard_map/all_gather | solution.py:127
  599.9 1.7 fusion.142
  601.7 1.7 select_dynamic-update-slice_fusion.2
  603.6 2.0 fusion.312
  606.2 2.2 fusion.69
  609.4 2.4 fusion.16
  612.7 1.3 gather_fusion.3
  616.2 14.5 %reduce-scatter.8.cloned.1.call-done = bf16[64,1024]{1,0:T(8,128)(2,1)} async-done(((bf16[64,4096]{1,0:T(8,128)(2,1)}), bf16[64,1024]{1,0:T(8,128)(2,1)}) %reduce-scatter.8.cloned.1.call-update) | async-done | bytes 131088 | tf_op jit(solution)/shard_map/reduce_scatter | solution.py:160
  631.6 1.3 collective-permute-start.1
  633.9 13.5 %all_gather.67 = bf16[64,4096]{1,0:T(8,128)(2,1)S(1)} all-gather(bf16[64,1024]{1,0:T(8,128)(2,1)S(1)} %broadcast_select_fusion.2), channel_id=1, replica_groups=mesh['section'=2,'blk'=16,'mp'=4] {'mp'}, dimensions={1}, use_global_device_ids=true | all-gather | bytes 655360 | tf_op jit(solution)/shard_map/all_gather | solution.py:105
  648.5 6.1 fusion.131
  654.6 23.8 %all-gather.2 = bf16[1024,1,1,128]{3,0,2,1:T(8,128)(2,1)S(1)} all-gather(bf16[64,1,1,128]{3,0,2,1:T(8,128)(2,1)S(1)} %slice.283), channel_id=4, replica_groups=mesh['section'=2,'blk'=16,'mp'=4] {'blk'}, dimensions={0}, use_global_device_ids=true | all-gather | bytes 278528 | tf_op jit(solution)/shard_map/all_gather | solution.py:128
  678.7 23.4 %all_gather.69 = bf16[1024,1,128]{2,0,1:T(8,128)(2,1)S(1)} all-gather(bf16[64,1,128]{2,0,1:T(8,128)(2,1)S(1)} %pad_maximum_fusion.2), channel_id=1, replica_groups=mesh['section'=2,'blk'=16,'mp'=4] {'blk'}, dimensions={0}, use_global_device_ids=true | all-gather | bytes 278528 | tf_op jit(solution)/shard_map/all_gather | solution.py:127
  702.1 1.7 fusion.141
  703.8 1.7 select_dynamic-update-slice_fusion.1
  705.7 2.4 fusion.313
  709.1 2.5 fusion.79
  712.1 2.4 fusion.19
  715.8 17.7 %reduce-scatter.10.cloned.1.call-done = bf16[64,1024]{1,0:T(8,128)(2,1)} async-done(((bf16[64,4096]{1,0:T(8,128)(2,1)}), bf16[64,1024]{1,0:T(8,128)(2,1)}) %reduce-scatter.10.cloned.1.call-update) | async-done | bytes 131088 | tf_op jit(solution)/shard_map/reduce_scatter | solution.py:160
  734.5 1.3 collective-permute-start.2
  737.7 13.4 %all_gather.70 = bf16[64,4096]{1,0:T(8,128)(2,1)S(1)} all-gather(bf16[64,1024]{1,0:T(8,128)(2,1)S(1)} %broadcast_select_fusion.1), channel_id=1, replica_groups=mesh['section'=2,'blk'=16,'mp'=4] {'mp'}, dimensions={1}, use_global_device_ids=true | all-gather | bytes 655360 | tf_op jit(solution)/shard_map/all_gather | solution.py:105
  752.1 6.1 fusion.134
  758.2 23.8 %all-gather.3 = bf16[1024,1,1,128]{3,0,2,1:T(8,128)(2,1)S(1)} all-gather(bf16[64,1,1,128]{3,0,2,1:T(8,128)(2,1)S(1)} %slice.282), channel_id=5, replica_groups=mesh['section'=2,'blk'=16,'mp'=4] {'blk'}, dimensions={0}, use_global_device_ids=true | all-gather | bytes 278528 | tf_op jit(solution)/shard_map/all_gather | solution.py:128
  782.3 23.2 %all_gather.72 = bf16[1024,1,128]{2,0,1:T(8,128)(2,1)S(1)} all-gather(bf16[64,1,128]{2,0,1:T(8,128)(2,1)S(1)} %pad_maximum_fusion.3), channel_id=1, replica_groups=mesh['section'=2,'blk'=16,'mp'=4] {'blk'}, dimensions={0}, use_global_device_ids=true | all-gather | bytes 278528 | tf_op jit(solution)/shard_map/all_gather | solution.py:127
  805.5 1.7 fusion.140
  807.2 1.7 select_dynamic-update-slice_fusion
  809.1 2.9 fusion.314
  812.0 1.3 fusion.10
  813.3 2.8 fusion.76
  816.2 2.4 fusion.22
  818.7 18.8 %reduce-scatter.12.cloned.1.call-done = bf16[64,1024]{1,0:T(8,128)(2,1)} async-done(((bf16[64,4096]{1,0:T(8,128)(2,1)}), bf16[64,1024]{1,0:T(8,128)(2,1)}) %reduce-scatter.12.cloned.1.call-update) | async-done | bytes 131088 | tf_op jit(solution)/shard_map/reduce_scatter | solution.py:160
  838.5 1.3 collective-permute-start.3
  840.9 1.2 copy.79
  842.2 1.2 copy.78
  844.1 12.8 %all_gather.73 = bf16[64,4096]{1,0:T(8,128)(2,1)S(1)} all-gather(bf16[64,1024]{1,0:T(8,128)(2,1)S(1)} %broadcast_select_fusion), channel_id=1, replica_groups=mesh['section'=2,'blk'=16,'mp'=4] {'mp'}, dimensions={1}, use_global_device_ids=true | all-gather | bytes 655360 | tf_op jit(solution)/shard_map/all_gather | solution.py:105
  857.9 6.1 fusion.137
  864.0 23.8 %all-gather.4 = bf16[1024,1,1,128]{3,0,2,1:T(8,128)(2,1)S(1)} all-gather(bf16[64,1,1,128]{3,0,2,1:T(8,128)(2,1)S(1)} %slice.281), channel_id=6, replica_groups=mesh['section'=2,'blk'=16,'mp'=4] {'blk'}, dimensions={0}, use_global_device_ids=true | all-gather | bytes 278528 | tf_op jit(solution)/shard_map/all_gather | solution.py:128
  888.0 23.3 %all_gather.75 = bf16[1024,1,128]{2,0,1:T(8,128)(2,1)S(1)} all-gather(bf16[64,1,128]{2,0,1:T(8,128)(2,1)S(1)} %pad_maximum_fusion.4), channel_id=1, replica_groups=mesh['section'=2,'blk'=16,'mp'=4] {'blk'}, dimensions={0}, use_global_device_ids=true | all-gather | bytes 278528 | tf_op jit(solution)/shard_map/all_gather | solution.py:127
  913.6 1.6 fusion.315
  915.2 1.3 fusion.11
  916.5 1.6 fusion.73
  918.9 2.4 fusion.25
  922.1 18.1 %reduce-scatter.14.cloned.1.call-done = bf16[64,1024]{1,0:T(8,128)(2,1)} async-done(((bf16[64,4096]{1,0:T(8,128)(2,1)}), bf16[64,1024]{1,0:T(8,128)(2,1)}) %reduce-scatter.14.cloned.1.call-update) | async-done | bytes 131088 | tf_op jit(solution)/shard_map/reduce_scatter | solution.py:160
  940.2 1.6 fusion.146
  (276 shorter events, 46.4 us)
Async XLA Ops:
  6.5 9.7 %copy-start = (bf16[5120,80]{0,1:T(8,128)(2,1)S(1)}, bf16[5120,80]{0,1:T(8,128)(2,1)}, u32[]{:S(2)}) copy-start(bf16[5120,80]{0,1:T(8,128)(2,1)} %param.15) | copy-start | bytes 2457604
  6.5 419.6 %all-gather.9.cloned.1.call-start = ((), (), s32[]{:S(2)}) async-start(), calls=%async_computation.5 | async-start | bytes 2228224 | tf_op jit(solution)/shard_map/all_gather | solution.py:74
  7.3 473.2 %all-gather.11.cloned.1.call-start = ((), (), s32[]{:S(2)}) async-start(), calls=%async_computation.6 | async-start | bytes 8912896 | tf_op jit(solution)/shard_map/all_gather | solution.py:73
  8.0 494.1 %all-gather.13.cloned.1.call-start = ((), (), s32[]{:S(2)}) async-start(), calls=%async_computation.7 | async-start | bytes 8912896 | tf_op jit(solution)/shard_map/all_gather | solution.py:75
  8.7 517.9 %reduce-scatter.6.cloned.1.call-start = ((), (), s32[]{:S(2)}) async-start(), calls=%async_computation.8 | async-start | bytes 655360 | tf_op jit(solution)/shard_map/reduce_scatter | solution.py:160
  16.2 5.2 copy-start.2
  21.4 385.4 %copy-start.25 = (s32[256]{0:T(256)S(1)}, s32[256]{0:T(256)}, u32[]{:S(2)}) copy-start(s32[256]{0:T(256)} %param.18) | copy-start | bytes 3076
  21.4 403.2 %slice-start.8 = ((s32[4096]{0:T(1024)}), s32[1024]{0:T(1024)S(1)}, s32[]{:S(2)}) async-start(s32[4096]{0:T(1024)} %param.19), calls=%async_computation.21 | async-start | bytes 8192 | tf_op jit(solution)/shard_map/slice | solution.py:149
  21.4 404.6 %copy-start.46 = (f32[64]{0:T(128)}, f32[64]{0:T(128)S(1)}, u32[]{:S(2)}) copy-start(f32[64]{0:T(128)S(1)} %get-tuple-element.74) | copy-start | bytes 772
  22.2 554.2 %copy-start.26 = (f32[64]{0:T(128)}, f32[64]{0:T(128)S(1)}, u32[]{:S(2)}) copy-start(f32[64]{0:T(128)S(1)} %multiply_exponential_fusion) | copy-start | bytes 772
  22.2 384.6 %copy-start.44 = (s32[64]{0:T(128)}, s32[64]{0:T(128)S(1)}, u32[]{:S(2)}) copy-start(s32[64]{0:T(128)S(1)} %iota_add_fusion.5) | copy-start | bytes 772
  22.3 384.5 %copy-start.29 = (s32[64]{0:T(128)}, s32[64]{0:T(128)S(1)}, u32[]{:S(2)}) copy-start(s32[64]{0:T(128)S(1)} %get-tuple-element.77) | copy-start | bytes 772
  22.3 403.8 %copy-start.40 = (f32[64]{0:T(128)}, f32[64]{0:T(128)S(1)}, u32[]{:S(2)}) copy-start(f32[64]{0:T(128)S(1)} %get-tuple-element.80) | copy-start | bytes 772
  22.3 403.8 %copy-start.42 = (f32[64]{0:T(128)}, f32[64]{0:T(128)S(1)}, u32[]{:S(2)}) copy-start(f32[64]{0:T(128)S(1)} %get-tuple-element.79) | copy-start | bytes 772
  22.3 384.5 %copy-start.32 = (s32[64]{0:T(128)}, s32[64]{0:T(128)S(1)}, u32[]{:S(2)}) copy-start(s32[64]{0:T(128)S(1)} %get-tuple-element.75) | copy-start | bytes 772
  22.3 384.5 %copy-start.34 = (s32[64]{0:T(128)}, s32[64]{0:T(128)S(1)}, u32[]{:S(2)}) copy-start(s32[64]{0:T(128)S(1)} %get-tuple-element.76) | copy-start | bytes 772
  22.3 403.7 %copy-start.36 = (f32[64]{0:T(128)}, f32[64]{0:T(128)S(1)}, u32[]{:S(2)}) copy-start(f32[64]{0:T(128)S(1)} %get-tuple-element.82) | copy-start | bytes 772
  22.4 403.7 %copy-start.38 = (f32[64]{0:T(128)}, f32[64]{0:T(128)S(1)}, u32[]{:S(2)}) copy-start(f32[64]{0:T(128)S(1)} %get-tuple-element.81) | copy-start | bytes 772
  406.7 24.1 %copy-start.4 = (f32[1,4096]{1,0:T(1,128)S(1)}, f32[1,4096]{1,0:T(1,128)}, u32[]{:S(2)}) copy-start(f32[1,4096]{1,0:T(1,128)} %param.20) | copy-start | bytes 49156
  411.0 20.7 %copy-start.11 = (bf16[64,1024]{1,0:T(8,128)(2,1)}, bf16[64,1024]{1,0:T(8,128)(2,1)S(1)}, u32[]{:S(2)}) copy-start(bf16[64,1024]{1,0:T(8,128)(2,1)S(1)} %fusion.63) | copy-start | bytes 393220
  424.6 7.4 copy-start.48
  426.1 5.6 copy-start.47
  480.5 11.8 %copy-start.49 = (f32[64]{0:T(128)S(1)}, f32[64]{0:T(128)}, u32[]{:S(2)}) copy-start(f32[64]{0:T(128)} %copy-done.48) | copy-start | bytes 772
  492.2 6.1 copy-start.23
  492.3 6.1 copy-start.24
  502.2 5.9 copy-start.51
  502.2 8.2 slice-start.9
  502.2 8.2 copy-start.30
  502.2 24.5 %copy-start.12 = (bf16[64,1024]{1,0:T(8,128)(2,1)S(1)}, bf16[64,1024]{1,0:T(8,128)(2,1)}, u32[]{:S(2)}) copy-start(bf16[64,1024]{1,0:T(8,128)(2,1)} %copy-done.11) | copy-start | bytes 393220
  502.2 28.6 %copy-start.50 = (pred[64]{0:T(512)(128)(4,1)S(1)}, pred[64]{0:T(512)(128)(4,1)}, u32[]{:S(2)}) copy-start(pred[64]{0:T(512)(128)(4,1)} %get-tuple-element.7) | copy-start | bytes 196
  508.0 122.6 %reduce-scatter.8.cloned.1.call-start = ((), (), s32[]{:S(2)}) async-start(), calls=%async_computation.9 | async-start | bytes 655360 | tf_op jit(solution)/shard_map/reduce_scatter | solution.py:160
  527.7 2.4 collective-permute-start
  531.9 14.5 %copy-start.7 = (bf16[64,1024]{1,0:T(8,128)(2,1)}, bf16[64,1024]{1,0:T(8,128)(2,1)S(1)}, u32[]{:S(2)}) copy-start(bf16[64,1024]{1,0:T(8,128)(2,1)S(1)} %fusion.65) | copy-start | bytes 393220
  546.4 29.9 %copy-start.43 = (f32[64]{0:T(128)S(1)}, f32[64]{0:T(128)}, u32[]{:S(2)}) copy-start(f32[64]{0:T(128)} %copy-done.42) | copy-start | bytes 772
  546.5 56.9 %copy-start.21 = (f32[64,64]{1,0:T(8,128)S(1)}, f32[64,64]{1,0:T(8,128)}, u32[]{:S(2)}) copy-start(f32[64,64]{1,0:T(8,128)} %get-tuple-element.51) | copy-start | bytes 49156
  546.5 56.9 %copy-start.22 = (f32[64,64]{1,0:T(8,128)S(1)}, f32[64,64]{1,0:T(8,128)}, u32[]{:S(2)}) copy-start(f32[64,64]{1,0:T(8,128)} %get-tuple-element.52) | copy-start | bytes 49156
  546.5 57.1 %copy-start.14 = (pred[64,2048]{1,0:T(8,128)(4,1)S(1)}, pred[64,2048]{1,0:T(8,128)(4,1)}, u32[]{:S(2)}) copy-start(pred[64,2048]{1,0:T(8,128)(4,1)} %compare_and_fusion.1) | copy-start | bytes 393220
  609.3 4.7 copy-start.55
  609.3 5.9 slice-start.10
  609.3 5.9 copy-start.56
  609.4 21.3 %copy-start.8 = (bf16[64,1024]{1,0:T(8,128)(2,1)S(1)}, bf16[64,1024]{1,0:T(8,128)(2,1)}, u32[]{:S(2)}) copy-start(bf16[64,1024]{1,0:T(8,128)(2,1)} %copy-done.7) | copy-start | bytes 393220
  611.8 121.7 %reduce-scatter.10.cloned.1.call-start = ((), (), s32[]{:S(2)}) async-start(), calls=%async_computation.10 | async-start | bytes 655360 | tf_op jit(solution)/shard_map/reduce_scatter | solution.py:160
  631.6 2.3 collective-permute-start.1
  633.9 14.6 %copy-start.6 = (bf16[64,1024]{1,0:T(8,128)(2,1)}, bf16[64,1024]{1,0:T(8,128)(2,1)S(1)}, u32[]{:S(2)}) copy-start(bf16[64,1024]{1,0:T(8,128)(2,1)S(1)} %broadcast_select_fusion.2) | copy-start | bytes 393220
  648.5 29.9 %copy-start.27 = (f32[64]{0:T(128)S(1)}, f32[64]{0:T(128)}, u32[]{:S(2)}) copy-start(f32[64]{0:T(128)} %copy-done.26) | copy-start | bytes 772
  648.5 29.9 %copy-start.41 = (f32[64]{0:T(128)S(1)}, f32[64]{0:T(128)}, u32[]{:S(2)}) copy-start(f32[64]{0:T(128)} %copy-done.40) | copy-start | bytes 772
  648.5 57.1 %copy-start.19 = (f32[64,64]{1,0:T(8,128)S(1)}, f32[64,64]{1,0:T(8,128)}, u32[]{:S(2)}) copy-start(f32[64,64]{1,0:T(8,128)} %get-tuple-element.53) | copy-start | bytes 49156
  648.5 57.1 %copy-start.20 = (f32[64,64]{1,0:T(8,128)S(1)}, f32[64,64]{1,0:T(8,128)}, u32[]{:S(2)}) copy-start(f32[64,64]{1,0:T(8,128)} %get-tuple-element.54) | copy-start | bytes 49156
  648.5 57.2 %copy-start.13 = (pred[64,3072]{1,0:T(8,128)(4,1)S(1)}, pred[64,3072]{1,0:T(8,128)(4,1)}, u32[]{:S(2)}) copy-start(pred[64,3072]{1,0:T(8,128)(4,1)} %compare_and_fusion) | copy-start | bytes 589828
  712.1 23.7 %copy-start.54 = (pred[64]{0:T(512)(128)(4,1)S(1)}, pred[64]{0:T(512)(128)(4,1)}, u32[]{:S(2)}) copy-start(pred[64]{0:T(512)(128)(4,1)} %get-tuple-element.9) | copy-start | bytes 196
  714.5 122.9 %reduce-scatter.12.cloned.1.call-start = ((), (), s32[]{:S(2)}) async-start(), calls=%async_computation.11 | async-start | bytes 655360 | tf_op jit(solution)/shard_map/reduce_scatter | solution.py:160
  734.5 2.5 collective-permute-start.2
  752.1 29.9 %copy-start.39 = (f32[64]{0:T(128)S(1)}, f32[64]{0:T(128)}, u32[]{:S(2)}) copy-start(f32[64]{0:T(128)} %copy-done.38) | copy-start | bytes 772
  752.1 56.9 %copy-start.17 = (f32[64,64]{1,0:T(8,128)S(1)}, f32[64,64]{1,0:T(8,128)}, u32[]{:S(2)}) copy-start(f32[64,64]{1,0:T(8,128)} %get-tuple-element.55) | copy-start | bytes 49156
  752.1 56.9 %copy-start.18 = (f32[64,64]{1,0:T(8,128)S(1)}, f32[64,64]{1,0:T(8,128)}, u32[]{:S(2)}) copy-start(f32[64,64]{1,0:T(8,128)} %get-tuple-element.56) | copy-start | bytes 49156
  752.1 57.0 %copy-start.3 = (pred[64,4096]{1,0:T(8,128)(4,1)S(1)}, pred[64,4096]{1,0:T(8,128)(4,1)}, u32[]{:S(2)}) copy-start(pred[64,4096]{1,0:T(8,128)(4,1)} %get-tuple-element.40) | copy-start | bytes 786436
  816.2 23.5 %copy-start.53 = (pred[64]{0:T(512)(128)(4,1)S(1)}, pred[64]{0:T(512)(128)(4,1)}, u32[]{:S(2)}) copy-start(pred[64]{0:T(512)(128)(4,1)} %get-tuple-element.6) | copy-start | bytes 196
  818.6 121.5 %reduce-scatter.14.cloned.1.call-start = ((), (), s32[]{:S(2)}) async-start(), calls=%async_computation.12 | async-start | bytes 655360 | tf_op jit(solution)/shard_map/reduce_scatter | solution.py:160
  838.5 4.9 collective-permute-start.3
  857.9 29.9 %copy-start.28 = (f32[64]{0:T(128)S(1)}, f32[64]{0:T(128)}, u32[]{:S(2)}) copy-start(f32[64]{0:T(128)} %copy-done.26) | copy-start | bytes 772
  857.9 29.8 %copy-start.37 = (f32[64]{0:T(128)S(1)}, f32[64]{0:T(128)}, u32[]{:S(2)}) copy-start(f32[64]{0:T(128)} %copy-done.36) | copy-start | bytes 772
  857.9 55.5 %copy-start.16 = (f32[64,64]{1,0:T(8,128)S(1)}, f32[64,64]{1,0:T(8,128)}, u32[]{:S(2)}) copy-start(f32[64,64]{1,0:T(8,128)} %get-tuple-element.42) | copy-start | bytes 49156
  918.9 21.3 %copy-start.10 = (bf16[64,1024]{1,0:T(8,128)(2,1)S(1)}, bf16[64,1024]{1,0:T(8,128)(2,1)}, u32[]{:S(2)}) copy-start(bf16[64,1024]{1,0:T(8,128)(2,1)} %copy-done.9) | copy-start | bytes 393220
  918.9 22.9 %copy-start.1 = (bf16[5120,80]{0,1:T(8,128)(2,1)S(1)}, bf16[5120,80]{0,1:T(8,128)(2,1)}, u32[]{:S(2)}) copy-start(bf16[5120,80]{0,1:T(8,128)(2,1)} %param.15) | copy-start | bytes 2457604
  (18 other events, 46.7 us)
Sparse Core Ops, SparseCore 0:
  9.5 47.7 all-gather.8
  59.5 74.0 all-gather.10
  135.7 81.8 all-gather.12
  508.1 18.4 reduce-scatter.5
  611.9 18.7 reduce-scatter.7
  714.6 18.8 reduce-scatter.9
  818.8 18.6 reduce-scatter.11
  921.4 18.7 reduce-scatter.13
where the time goes:
time: 957 us; the launch traced here: 949 us
  blocking collectives  685 us (72%)
  waiting for transfers between devices  87 us (9%)
  matrix products  81.5 us (9%)
  other arithmetic  37.5 us (4%)
  local copies, waits for them, and re-layouts  37.3 us (4%)
  between operations  15.1 us (2%)
    psum x1, blocking collectives, local(): merged_full = lax.psum(partial_merge, ('blk', 'mp')).astype(jnp.bfloat16)  383 us
    all_gather x5, blocking collectives, local(): lax.all_gather(new_values, 'blk', axis=0, tiled=True)  119 us
    all_gather x5, blocking collectives, local(): lax.all_gather(new_keys, 'blk', axis=0, tiled=True)  114 us
    reduce_scatter x5, waiting for transfers between devices, local(): lax.psum_scatter(term.astype(jnp.bfloat16), 'mp', scatter_dimension=1, ti...  84.4 us
    all_gather x5, blocking collectives, local(): features = lax.all_gather(incoming, 'mp', axis=1, tiled=True)  66.5 us
    dot_general x5, matrix products, local(): jnp.dot(normx, query_full, preferred_element_type=jnp.float32)  30.4 us
  transfers between devices with their start and end apart: 12, of which 6 were waited for; matrix products, arithmetic and copies ran while one was open for 7% of the time, Pallas kernels for 0%

commit v1 on v0

--- a/solution.py
+++ b/solution.py
@@ -66,7 +66,7 @@
         jnp.dot(normed, merge_first, preferred_element_type=jnp.float32), approximate=False
     ).astype(jnp.bfloat16)
     partial_merge = jnp.dot(inner, merge_second, preferred_element_type=jnp.float32)
-    merged_full = lax.psum(partial_merge, ("blk", "mp")).astype(jnp.bfloat16)
+    merged_full = lax.psum(lax.psum(partial_merge, "blk"), "mp").astype(jnp.bfloat16)
     merged_mine = lax.dynamic_slice_in_dim(merged_full, model_index * slice_width, slice_width, 1)
     visual_all = lax.all_gather(merged_mine, "section", axis=0, tiled=True)
     query_full, keyval_full, out_full = (

time: 957 us -> 770 us (0.80)
  blocking collectives: 685 us -> 346 us
  waiting for transfers between devices: 87 us -> 239 us
    psum x1, blocking collectives: 383 us -> 43 us  [local(): lax.psum(lax.psum(partial_merge, 'blk'), 'mp').astype(jnp.bfloat16)]
    psum x0 -> x1, waiting for transfers between devices: none -> 86.1 us  [local(): lax.psum(partial_merge, 'blk')]
    all_gather x1, waiting for transfers between devices: 0.02 us -> 58.3 us  [local(): lax.all_gather(out_weight, 'blk', axis=2, tiled=True)]
  transfers between devices with their start and end apart: 12 -> 13, of which waited for: 6 -> 8; matrix products, arithmetic and copies ran while one was open for 7% -> 7% of each run, Pallas kernels for 0% -> 0%
where the time goes in v1:
time: 770 us; the launch traced here: 762 us
  blocking collectives  346 us (45%)
  waiting for transfers between devices  239 us (31%)
  matrix products  82 us (11%)
  other arithmetic  37.5 us (5%)
  local copies, waits for them, and re-layouts  37 us (5%)
  between operations  14.8 us (2%)
    all_gather x5, blocking collectives, local(): lax.all_gather(new_values, 'blk', axis=0, tiled=True)  117 us
    all_gather x5, blocking collectives, local(): lax.all_gather(new_keys, 'blk', axis=0, tiled=True)  117 us
    reduce_scatter x5, waiting for transfers between devices, local(): lax.psum_scatter(term.astype(jnp.bfloat16), 'mp', scatter_dimension=1, ti...  87.5 us
    psum x1, waiting for transfers between devices, local(): lax.psum(partial_merge, 'blk')  86.1 us
    all_gather x5, blocking collectives, local(): features = lax.all_gather(incoming, 'mp', axis=1, tiled=True)  66 us
    all_gather x1, waiting for transfers between devices, local(): lax.all_gather(out_weight, 'blk', axis=2, tiled=True)  58.3 us
    psum x1, blocking collectives, local(): lax.psum(lax.psum(partial_merge, 'blk'), 'mp').astype(jnp.bfloat16)  43 us
    dot_general x5, matrix products, local(): jnp.dot(normx, query_full, preferred_element_type=jnp.float32)  30.7 us
  transfers between devices with their start and end apart: 13, of which 8 were waited for; matrix products, arithmetic and copies ran while one was open for 7% of the time, Pallas kernels for 0%

profile of v1, /device:TPU:0, one launch (start us, length us, event | category | flops | bytes accessed | tf_op | source)
XLA Modules:
  0.0 761.7 jit_solution(9915978230422649825)
XLA Ops:
  6.5 2.9 reshape.1266
  12.0 1.9 copy.38
  14.1 5.4 fusion.210
  24.7 1.3 multiply_cosine_fusion
  26.0 86.1 %all-reduce.3.cloned.1.call-done = f32[128,4096]{1,0:T(8,128)} async-done(((f32[128,4096]{1,0:T(8,128)}), f32[128,4096]{1,0:T(8,128)}) %all-reduce.3.cloned.1.call-update) | async-done | bytes 2097168 | tf_op jit(solution)/shard_map/psum | solution.py:69
  112.1 43.0 %all-reduce.4 = bf16[128,4096]{1,0:T(8,128)(2,1)S(1)} all-reduce(f32[128,4096]{1,0:T(8,128)} %all-reduce.3.cloned.1.call-done), channel_id=1, replica_groups=mesh['section'=2,'blk'=16,'mp'=4] {'mp'}, use_global_device_ids=true, to_apply=%region_4.5 | all-reduce | flops 524288 | bytes 3145728 | tf_op jit(solution)/shard_map/psum | solution.py:69
  155.2 2.2 all_gather.57
  158.6 13.0 %all_gather.58 = bf16[64,4096]{1,0:T(8,128)(2,1)S(1)} all-gather(bf16[64,1024]{1,0:T(8,128)(2,1)S(1)} %fusion.63), channel_id=1, replica_groups=mesh['section'=2,'blk'=16,'mp'=4] {'mp'}, dimensions={1}, use_global_device_ids=true | all-gather | bytes 655360 | tf_op jit(solution)/shard_map/all_gather | solution.py:105
  171.8 4.7 copy.37
  177.7 24.0 %all_gather.61 = bf16[1024,1,128]{2,0,1:T(8,128)(2,1)S(1)} all-gather(bf16[64,1,128]{2,0,1:T(8,128)(2,1)S(1)} %pad_maximum_fusion), channel_id=1, replica_groups=mesh['section'=2,'blk'=16,'mp'=4] {'blk'}, dimensions={0}, use_global_device_ids=true | all-gather | bytes 278528 | tf_op jit(solution)/shard_map/all_gather | solution.py:127
  201.7 22.3 %all-gather = bf16[1024,1,1,128]{3,0,2,1:T(8,128)(2,1)S(1)} all-gather(bf16[64,1,1,128]{3,0,2,1:T(8,128)(2,1)S(1)} %slice.285), channel_id=2, replica_groups=mesh['section'=2,'blk'=16,'mp'=4] {'blk'}, dimensions={0}, use_global_device_ids=true | all-gather | bytes 278528 | tf_op jit(solution)/shard_map/all_gather | solution.py:128
  227.7 5.2 all-gather.11.cloned.1.call-done
  233.0 11.4 %copy.31 = bf16[1024,4096]{1,0:T(8,128)(2,1)} copy(bf16[1024,4096]{0,1:T(8,128)(2,1)} %bitcast.333) | data formatting | bytes 16777216 | tf_op jit(solution)/shard_map/dot_general | solution.py:113
  244.4 6.3 fusion.125
  250.9 1.5 fusion.311
  253.0 1.5 fusion.72
  254.6 58.3 %all-gather.13.cloned.1.call-done = bf16[1,1024,4096]{2,1,0:T(8,128)(2,1)} async-done(((bf16[1,1024,256]{2,1,0:T(8,128)(2,1)}), bf16[1,1024,4096]{2,1,0:T(8,128)(2,1)}) %all-gather.13.cloned.1.call-update) | async-done | bytes 8388624 | tf_op jit(solution)/shard_map/all_gather | solution.py:75
  312.9 5.8 fusion.13
  321.9 18.1 %reduce-scatter.6.cloned.1.call-done = bf16[64,1024]{1,0:T(8,128)(2,1)} async-done(((bf16[64,4096]{1,0:T(8,128)(2,1)}), bf16[64,1024]{1,0:T(8,128)(2,1)}) %reduce-scatter.6.cloned.1.call-update) | async-done | bytes 131088 | tf_op jit(solution)/shard_map/reduce_scatter | solution.py:160
  341.0 1.3 collective-permute-start
  345.3 13.5 %all_gather.64 = bf16[64,4096]{1,0:T(8,128)(2,1)S(1)} all-gather(bf16[64,1024]{1,0:T(8,128)(2,1)S(1)} %fusion.65), channel_id=1, replica_groups=mesh['section'=2,'blk'=16,'mp'=4] {'mp'}, dimensions={1}, use_global_device_ids=true | all-gather | bytes 655360 | tf_op jit(solution)/shard_map/all_gather | solution.py:105
  359.8 6.1 fusion.128
  365.9 23.7 %all-gather.1 = bf16[1024,1,1,128]{3,0,2,1:T(8,128)(2,1)S(1)} all-gather(bf16[64,1,1,128]{3,0,2,1:T(8,128)(2,1)S(1)} %slice.284), channel_id=3, replica_groups=mesh['section'=2,'blk'=16,'mp'=4] {'blk'}, dimensions={0}, use_global_device_ids=true | all-gather | bytes 278528 | tf_op jit(solution)/shard_map/all_gather | solution.py:128
  389.9 23.3 %all_gather.66 = bf16[1024,1,128]{2,0,1:T(8,128)(2,1)S(1)} all-gather(bf16[64,1,128]{2,0,1:T(8,128)(2,1)S(1)} %pad_maximum_fusion.1), channel_id=1, replica_groups=mesh['section'=2,'blk'=16,'mp'=4] {'blk'}, dimensions={0}, use_global_device_ids=true | all-gather | bytes 278528 | tf_op jit(solution)/shard_map/all_gather | solution.py:127
  413.2 1.7 fusion.142
  414.9 1.7 select_dynamic-update-slice_fusion.2
  416.8 2.0 fusion.312
  419.5 2.2 fusion.69
  422.6 2.4 fusion.16
  426.0 1.3 gather_fusion.3
  428.8 15.1 %reduce-scatter.8.cloned.1.call-done = bf16[64,1024]{1,0:T(8,128)(2,1)} async-done(((bf16[64,4096]{1,0:T(8,128)(2,1)}), bf16[64,1024]{1,0:T(8,128)(2,1)}) %reduce-scatter.8.cloned.1.call-update) | async-done | bytes 131088 | tf_op jit(solution)/shard_map/reduce_scatter | solution.py:160
  444.8 1.3 collective-permute-start.1
  447.4 13.4 %all_gather.67 = bf16[64,4096]{1,0:T(8,128)(2,1)S(1)} all-gather(bf16[64,1024]{1,0:T(8,128)(2,1)S(1)} %broadcast_select_fusion.2), channel_id=1, replica_groups=mesh['section'=2,'blk'=16,'mp'=4] {'mp'}, dimensions={1}, use_global_device_ids=true | all-gather | bytes 655360 | tf_op jit(solution)/shard_map/all_gather | solution.py:105
  461.9 6.1 fusion.131
  468.0 23.7 %all-gather.2 = bf16[1024,1,1,128]{3,0,2,1:T(8,128)(2,1)S(1)} all-gather(bf16[64,1,1,128]{3,0,2,1:T(8,128)(2,1)S(1)} %slice.283), channel_id=4, replica_groups=mesh['section'=2,'blk'=16,'mp'=4] {'blk'}, dimensions={0}, use_global_device_ids=true | all-gather | bytes 278528 | tf_op jit(solution)/shard_map/all_gather | solution.py:128
  492.0 23.5 %all_gather.69 = bf16[1024,1,128]{2,0,1:T(8,128)(2,1)S(1)} all-gather(bf16[64,1,128]{2,0,1:T(8,128)(2,1)S(1)} %pad_maximum_fusion.2), channel_id=1, replica_groups=mesh['section'=2,'blk'=16,'mp'=4] {'blk'}, dimensions={0}, use_global_device_ids=true | all-gather | bytes 278528 | tf_op jit(solution)/shard_map/all_gather | solution.py:127
  515.4 1.7 fusion.141
  517.2 1.7 select_dynamic-update-slice_fusion.1
  519.1 2.4 fusion.313
  522.5 2.5 fusion.79
  525.5 2.4 fusion.19
  529.1 17.6 %reduce-scatter.10.cloned.1.call-done = bf16[64,1024]{1,0:T(8,128)(2,1)} async-done(((bf16[64,4096]{1,0:T(8,128)(2,1)}), bf16[64,1024]{1,0:T(8,128)(2,1)}) %reduce-scatter.10.cloned.1.call-update) | async-done | bytes 131088 | tf_op jit(solution)/shard_map/reduce_scatter | solution.py:160
  547.8 1.3 collective-permute-start.2
  550.9 13.3 %all_gather.70 = bf16[64,4096]{1,0:T(8,128)(2,1)S(1)} all-gather(bf16[64,1024]{1,0:T(8,128)(2,1)S(1)} %broadcast_select_fusion.1), channel_id=1, replica_groups=mesh['section'=2,'blk'=16,'mp'=4] {'mp'}, dimensions={1}, use_global_device_ids=true | all-gather | bytes 655360 | tf_op jit(solution)/shard_map/all_gather | solution.py:105
  565.4 6.1 fusion.134
  571.5 23.8 %all-gather.3 = bf16[1024,1,1,128]{3,0,2,1:T(8,128)(2,1)S(1)} all-gather(bf16[64,1,1,128]{3,0,2,1:T(8,128)(2,1)S(1)} %slice.282), channel_id=5, replica_groups=mesh['section'=2,'blk'=16,'mp'=4] {'blk'}, dimensions={0}, use_global_device_ids=true | all-gather | bytes 278528 | tf_op jit(solution)/shard_map/all_gather | solution.py:128
  595.5 23.2 %all_gather.72 = bf16[1024,1,128]{2,0,1:T(8,128)(2,1)S(1)} all-gather(bf16[64,1,128]{2,0,1:T(8,128)(2,1)S(1)} %pad_maximum_fusion.3), channel_id=1, replica_groups=mesh['section'=2,'blk'=16,'mp'=4] {'blk'}, dimensions={0}, use_global_device_ids=true | all-gather | bytes 278528 | tf_op jit(solution)/shard_map/all_gather | solution.py:127
  618.8 1.7 fusion.140
  620.5 1.7 select_dynamic-update-slice_fusion
  622.4 2.9 fusion.314
  625.3 1.3 fusion.10
  626.5 2.8 fusion.76
  629.5 2.4 fusion.22
  631.9 18.8 %reduce-scatter.12.cloned.1.call-done = bf16[64,1024]{1,0:T(8,128)(2,1)} async-done(((bf16[64,4096]{1,0:T(8,128)(2,1)}), bf16[64,1024]{1,0:T(8,128)(2,1)}) %reduce-scatter.12.cloned.1.call-update) | async-done | bytes 131088 | tf_op jit(solution)/shard_map/reduce_scatter | solution.py:160
  651.7 1.3 collective-permute-start.3
  657.3 12.8 %all_gather.73 = bf16[64,4096]{1,0:T(8,128)(2,1)S(1)} all-gather(bf16[64,1024]{1,0:T(8,128)(2,1)S(1)} %broadcast_select_fusion), channel_id=1, replica_groups=mesh['section'=2,'blk'=16,'mp'=4] {'mp'}, dimensions={1}, use_global_device_ids=true | all-gather | bytes 655360 | tf_op jit(solution)/shard_map/all_gather | solution.py:105
  671.2 6.1 fusion.137
  677.2 23.7 %all-gather.4 = bf16[1024,1,1,128]{3,0,2,1:T(8,128)(2,1)S(1)} all-gather(bf16[64,1,1,128]{3,0,2,1:T(8,128)(2,1)S(1)} %slice.281), channel_id=6, replica_groups=mesh['section'=2,'blk'=16,'mp'=4] {'blk'}, dimensions={0}, use_global_device_ids=true | all-gather | bytes 278528 | tf_op jit(solution)/shard_map/all_gather | solution.py:128
  701.3 23.3 %all_gather.75 = bf16[1024,1,128]{2,0,1:T(8,128)(2,1)S(1)} all-gather(bf16[64,1,128]{2,0,1:T(8,128)(2,1)S(1)} %pad_maximum_fusion.4), channel_id=1, replica_groups=mesh['section'=2,'blk'=16,'mp'=4] {'blk'}, dimensions={0}, use_global_device_ids=true | all-gather | bytes 278528 | tf_op jit(solution)/shard_map/all_gather | solution.py:127
  726.8 1.6 fusion.315
  729.7 1.6 fusion.73
  732.1 2.4 fusion.25
  735.3 18.0 %reduce-scatter.14.cloned.1.call-done = bf16[64,1024]{1,0:T(8,128)(2,1)} async-done(((bf16[64,4096]{1,0:T(8,128)(2,1)}), bf16[64,1024]{1,0:T(8,128)(2,1)}) %reduce-scatter.14.cloned.1.call-update) | async-done | bytes 131088 | tf_op jit(solution)/shard_map/reduce_scatter | solution.py:160
  753.4 1.6 fusion.146
  (281 shorter events, 49.6 us)
Async XLA Ops:
  6.5 7.5 copy-start
  6.5 105.6 %all-reduce.3.cloned.1.call-start = ((), (), s32[]{:S(2)}) async-start(), calls=%async_computation.5 | async-start | bytes 4194304 | tf_op jit(solution)/shard_map/psum | solution.py:69
  14.0 7.6 %copy-start.2 = (s32[4096]{0:T(1024)S(1)}, s32[4096]{0:T(1024)}, u32[]{:S(2)}) copy-start(s32[4096]{0:T(1024)} %param.19) | copy-start | bytes 49156
  14.0 9.7 %copy-start.25 = (s32[256]{0:T(256)S(1)}, s32[256]{0:T(256)}, u32[]{:S(2)}) copy-start(s32[256]{0:T(256)} %param.18) | copy-start | bytes 3076
  14.0 10.5 %slice-start.8 = ((s32[4096]{0:T(1024)}), s32[1024]{0:T(1024)S(1)}, s32[]{:S(2)}) async-start(s32[4096]{0:T(1024)} %param.19), calls=%async_computation.22 | async-start | bytes 8192 | tf_op jit(solution)/shard_map/slice | solution.py:149
  19.4 138.0 %copy-start.26 = (s32[256]{0:T(256)S(1)}, s32[256]{0:T(256)}, u32[]{:S(2)}) copy-start(s32[256]{0:T(256)} %param.18) | copy-start | bytes 3076
  19.4 152.4 %all-gather.9.cloned.1.call-start = ((), (), s32[]{:S(2)}) async-start(), calls=%async_computation.6 | async-start | bytes 2228224 | tf_op jit(solution)/shard_map/all_gather | solution.py:74
  20.2 212.8 %all-gather.11.cloned.1.call-start = ((), (), s32[]{:S(2)}) async-start(), calls=%async_computation.7 | async-start | bytes 8912896 | tf_op jit(solution)/shard_map/all_gather | solution.py:73
  20.9 292.0 %all-gather.13.cloned.1.call-start = ((), (), s32[]{:S(2)}) async-start(), calls=%async_computation.8 | async-start | bytes 8912896 | tf_op jit(solution)/shard_map/all_gather | solution.py:75
  21.5 318.4 %reduce-scatter.6.cloned.1.call-start = ((), (), s32[]{:S(2)}) async-start(), calls=%async_computation.9 | async-start | bytes 655360 | tf_op jit(solution)/shard_map/reduce_scatter | solution.py:160
  21.6 133.5 %copy-start.47 = (f32[64]{0:T(128)}, f32[64]{0:T(128)S(1)}, u32[]{:S(2)}) copy-start(f32[64]{0:T(128)S(1)} %get-tuple-element.74) | copy-start | bytes 772
  22.4 367.2 %copy-start.27 = (f32[64]{0:T(128)}, f32[64]{0:T(128)S(1)}, u32[]{:S(2)}) copy-start(f32[64]{0:T(128)S(1)} %multiply_exponential_fusion) | copy-start | bytes 772
  22.4 132.7 %copy-start.45 = (s32[64]{0:T(128)}, s32[64]{0:T(128)S(1)}, u32[]{:S(2)}) copy-start(s32[64]{0:T(128)S(1)} %iota_add_fusion.5) | copy-start | bytes 772
  22.5 154.1 %copy-start.30 = (s32[64]{0:T(128)}, s32[64]{0:T(128)S(1)}, u32[]{:S(2)}) copy-start(s32[64]{0:T(128)S(1)} %get-tuple-element.77) | copy-start | bytes 772
  22.5 132.6 %copy-start.41 = (f32[64]{0:T(128)}, f32[64]{0:T(128)S(1)}, u32[]{:S(2)}) copy-start(f32[64]{0:T(128)S(1)} %get-tuple-element.80) | copy-start | bytes 772
  22.5 132.6 %copy-start.43 = (f32[64]{0:T(128)}, f32[64]{0:T(128)S(1)}, u32[]{:S(2)}) copy-start(f32[64]{0:T(128)S(1)} %get-tuple-element.79) | copy-start | bytes 772
  22.5 132.6 %copy-start.33 = (s32[64]{0:T(128)}, s32[64]{0:T(128)S(1)}, u32[]{:S(2)}) copy-start(s32[64]{0:T(128)S(1)} %get-tuple-element.75) | copy-start | bytes 772
  22.5 132.6 %copy-start.35 = (s32[64]{0:T(128)}, s32[64]{0:T(128)S(1)}, u32[]{:S(2)}) copy-start(s32[64]{0:T(128)S(1)} %get-tuple-element.76) | copy-start | bytes 772
  22.6 132.6 %copy-start.37 = (f32[64]{0:T(128)}, f32[64]{0:T(128)S(1)}, u32[]{:S(2)}) copy-start(f32[64]{0:T(128)S(1)} %get-tuple-element.82) | copy-start | bytes 772
  22.6 132.6 %copy-start.39 = (f32[64]{0:T(128)}, f32[64]{0:T(128)S(1)}, u32[]{:S(2)}) copy-start(f32[64]{0:T(128)S(1)} %get-tuple-element.81) | copy-start | bytes 772
  155.2 21.4 %copy-start.4 = (f32[1,4096]{1,0:T(1,128)S(1)}, f32[1,4096]{1,0:T(1,128)}, u32[]{:S(2)}) copy-start(f32[1,4096]{1,0:T(1,128)} %param.20) | copy-start | bytes 49156
  158.6 43.1 %copy-start.11 = (bf16[64,1024]{1,0:T(8,128)(2,1)}, bf16[64,1024]{1,0:T(8,128)(2,1)S(1)}, u32[]{:S(2)}) copy-start(bf16[64,1024]{1,0:T(8,128)(2,1)S(1)} %fusion.63) | copy-start | bytes 393220
  158.6 18.8 %copy-start.48 = (f32[64]{0:T(128)S(1)}, f32[64]{0:T(128)}, u32[]{:S(2)}) copy-start(f32[64]{0:T(128)} %copy-done.47) | copy-start | bytes 772
  171.8 5.6 copy-start.49
  233.0 11.4 %copy-start.50 = (f32[64]{0:T(128)S(1)}, f32[64]{0:T(128)}, u32[]{:S(2)}) copy-start(f32[64]{0:T(128)} %copy-done.49) | copy-start | bytes 772
  244.4 6.3 copy-start.23
  244.4 6.3 copy-start.24
  312.9 5.9 copy-start.52
  312.9 8.2 %slice-start.9 = ((s32[4096]{0:T(1024)}), s32[2048]{0:T(1024)S(1)}, s32[]{:S(2)}) async-start(s32[4096]{0:T(1024)} %param.19), calls=%async_computation.23 | async-start | bytes 16384 | tf_op jit(solution)/shard_map/slice | solution.py:149
  312.9 8.2 %copy-start.31 = (s32[64]{0:T(128)S(1)}, s32[64]{0:T(128)}, u32[]{:S(2)}) copy-start(s32[64]{0:T(128)} %copy-done.30) | copy-start | bytes 772
  312.9 27.1 %copy-start.12 = (bf16[64,1024]{1,0:T(8,128)(2,1)S(1)}, bf16[64,1024]{1,0:T(8,128)(2,1)}, u32[]{:S(2)}) copy-start(bf16[64,1024]{1,0:T(8,128)(2,1)} %copy-done.11) | copy-start | bytes 393220
  312.9 31.2 %copy-start.51 = (pred[64]{0:T(512)(128)(4,1)S(1)}, pred[64]{0:T(512)(128)(4,1)}, u32[]{:S(2)}) copy-start(pred[64]{0:T(512)(128)(4,1)} %get-tuple-element.7) | copy-start | bytes 196
  318.7 125.1 %reduce-scatter.8.cloned.1.call-start = ((), (), s32[]{:S(2)}) async-start(), calls=%async_computation.10 | async-start | bytes 655360 | tf_op jit(solution)/shard_map/reduce_scatter | solution.py:160
  341.0 2.4 collective-permute-start
  345.2 14.5 %copy-start.7 = (bf16[64,1024]{1,0:T(8,128)(2,1)}, bf16[64,1024]{1,0:T(8,128)(2,1)S(1)}, u32[]{:S(2)}) copy-start(bf16[64,1024]{1,0:T(8,128)(2,1)S(1)} %fusion.65) | copy-start | bytes 393220
  359.8 29.9 %copy-start.44 = (f32[64]{0:T(128)S(1)}, f32[64]{0:T(128)}, u32[]{:S(2)}) copy-start(f32[64]{0:T(128)} %copy-done.43) | copy-start | bytes 772
  359.8 56.9 %copy-start.21 = (f32[64,64]{1,0:T(8,128)S(1)}, f32[64,64]{1,0:T(8,128)}, u32[]{:S(2)}) copy-start(f32[64,64]{1,0:T(8,128)} %get-tuple-element.51) | copy-start | bytes 49156
  359.8 56.9 %copy-start.22 = (f32[64,64]{1,0:T(8,128)S(1)}, f32[64,64]{1,0:T(8,128)}, u32[]{:S(2)}) copy-start(f32[64,64]{1,0:T(8,128)} %get-tuple-element.52) | copy-start | bytes 49156
  359.8 57.0 %copy-start.14 = (pred[64,2048]{1,0:T(8,128)(4,1)S(1)}, pred[64,2048]{1,0:T(8,128)(4,1)}, u32[]{:S(2)}) copy-start(pred[64,2048]{1,0:T(8,128)(4,1)} %compare_and_fusion.1) | copy-start | bytes 393220
  422.6 21.3 %copy-start.8 = (bf16[64,1024]{1,0:T(8,128)(2,1)S(1)}, bf16[64,1024]{1,0:T(8,128)(2,1)}, u32[]{:S(2)}) copy-start(bf16[64,1024]{1,0:T(8,128)(2,1)} %copy-done.7) | copy-start | bytes 393220
  422.6 23.5 %copy-start.56 = (pred[64]{0:T(512)(128)(4,1)S(1)}, pred[64]{0:T(512)(128)(4,1)}, u32[]{:S(2)}) copy-start(pred[64]{0:T(512)(128)(4,1)} %get-tuple-element.8) | copy-start | bytes 196
  425.0 121.7 %reduce-scatter.10.cloned.1.call-start = ((), (), s32[]{:S(2)}) async-start(), calls=%async_computation.11 | async-start | bytes 655360 | tf_op jit(solution)/shard_map/reduce_scatter | solution.py:160
  444.8 2.5 collective-permute-start.1
  447.3 14.4 %copy-start.6 = (bf16[64,1024]{1,0:T(8,128)(2,1)}, bf16[64,1024]{1,0:T(8,128)(2,1)S(1)}, u32[]{:S(2)}) copy-start(bf16[64,1024]{1,0:T(8,128)(2,1)S(1)} %broadcast_select_fusion.2) | copy-start | bytes 393220
  461.8 29.9 %copy-start.28 = (f32[64]{0:T(128)S(1)}, f32[64]{0:T(128)}, u32[]{:S(2)}) copy-start(f32[64]{0:T(128)} %copy-done.27) | copy-start | bytes 772
  461.8 29.9 %copy-start.42 = (f32[64]{0:T(128)S(1)}, f32[64]{0:T(128)}, u32[]{:S(2)}) copy-start(f32[64]{0:T(128)} %copy-done.41) | copy-start | bytes 772
  461.8 57.1 %copy-start.19 = (f32[64,64]{1,0:T(8,128)S(1)}, f32[64,64]{1,0:T(8,128)}, u32[]{:S(2)}) copy-start(f32[64,64]{1,0:T(8,128)} %get-tuple-element.53) | copy-start | bytes 49156
  461.8 57.1 %copy-start.20 = (f32[64,64]{1,0:T(8,128)S(1)}, f32[64,64]{1,0:T(8,128)}, u32[]{:S(2)}) copy-start(f32[64,64]{1,0:T(8,128)} %get-tuple-element.54) | copy-start | bytes 49156
  461.9 57.2 %copy-start.13 = (pred[64,3072]{1,0:T(8,128)(4,1)S(1)}, pred[64,3072]{1,0:T(8,128)(4,1)}, u32[]{:S(2)}) copy-start(pred[64,3072]{1,0:T(8,128)(4,1)} %compare_and_fusion) | copy-start | bytes 589828
  525.5 23.6 %copy-start.55 = (pred[64]{0:T(512)(128)(4,1)S(1)}, pred[64]{0:T(512)(128)(4,1)}, u32[]{:S(2)}) copy-start(pred[64]{0:T(512)(128)(4,1)} %get-tuple-element.9) | copy-start | bytes 196
  527.9 122.8 %reduce-scatter.12.cloned.1.call-start = ((), (), s32[]{:S(2)}) async-start(), calls=%async_computation.12 | async-start | bytes 655360 | tf_op jit(solution)/shard_map/reduce_scatter | solution.py:160
  547.8 2.5 collective-permute-start.2
  565.3 29.9 %copy-start.40 = (f32[64]{0:T(128)S(1)}, f32[64]{0:T(128)}, u32[]{:S(2)}) copy-start(f32[64]{0:T(128)} %copy-done.39) | copy-start | bytes 772
  565.3 56.9 %copy-start.17 = (f32[64,64]{1,0:T(8,128)S(1)}, f32[64,64]{1,0:T(8,128)}, u32[]{:S(2)}) copy-start(f32[64,64]{1,0:T(8,128)} %get-tuple-element.55) | copy-start | bytes 49156
  565.3 56.9 %copy-start.18 = (f32[64,64]{1,0:T(8,128)S(1)}, f32[64,64]{1,0:T(8,128)}, u32[]{:S(2)}) copy-start(f32[64,64]{1,0:T(8,128)} %get-tuple-element.56) | copy-start | bytes 49156
  565.3 57.0 %copy-start.3 = (pred[64,4096]{1,0:T(8,128)(4,1)S(1)}, pred[64,4096]{1,0:T(8,128)(4,1)}, u32[]{:S(2)}) copy-start(pred[64,4096]{1,0:T(8,128)(4,1)} %get-tuple-element.40) | copy-start | bytes 786436
  629.5 23.6 %copy-start.54 = (pred[64]{0:T(512)(128)(4,1)S(1)}, pred[64]{0:T(512)(128)(4,1)}, u32[]{:S(2)}) copy-start(pred[64]{0:T(512)(128)(4,1)} %get-tuple-element.6) | copy-start | bytes 196
  631.9 121.5 %reduce-scatter.14.cloned.1.call-start = ((), (), s32[]{:S(2)}) async-start(), calls=%async_computation.13 | async-start | bytes 655360 | tf_op jit(solution)/shard_map/reduce_scatter | solution.py:160
  651.7 4.9 collective-permute-start.3
  671.1 29.8 %copy-start.29 = (f32[64]{0:T(128)S(1)}, f32[64]{0:T(128)}, u32[]{:S(2)}) copy-start(f32[64]{0:T(128)} %copy-done.27) | copy-start | bytes 772
  671.1 29.8 %copy-start.38 = (f32[64]{0:T(128)S(1)}, f32[64]{0:T(128)}, u32[]{:S(2)}) copy-start(f32[64]{0:T(128)} %copy-done.37) | copy-start | bytes 772
  671.2 55.5 %copy-start.16 = (f32[64,64]{1,0:T(8,128)S(1)}, f32[64,64]{1,0:T(8,128)}, u32[]{:S(2)}) copy-start(f32[64,64]{1,0:T(8,128)} %get-tuple-element.42) | copy-start | bytes 49156
  732.1 21.2 %copy-start.10 = (bf16[64,1024]{1,0:T(8,128)(2,1)S(1)}, bf16[64,1024]{1,0:T(8,128)(2,1)}, u32[]{:S(2)}) copy-start(bf16[64,1024]{1,0:T(8,128)(2,1)} %copy-done.9) | copy-start | bytes 393220
  732.1 22.8 %copy-start.1 = (bf16[5120,80]{0,1:T(8,128)(2,1)S(1)}, bf16[5120,80]{0,1:T(8,128)(2,1)}, u32[]{:S(2)}) copy-start(bf16[5120,80]{0,1:T(8,128)(2,1)} %param.15) | copy-start | bytes 2457604
  (20 other events, 57.8 us)
Sparse Core Ops, SparseCore 0:
  19.6 92.4 all-reduce.2
  114.5 44.1 all-gather.8
  161.1 71.8 all-gather.10
  235.2 77.6 all-gather.12
  318.8 21.0 reduce-scatter.5
  425.1 18.6 reduce-scatter.7
  528.0 18.7 reduce-scatter.9
  632.0 18.6 reduce-scatter.11
  734.6 18.6 reduce-scatter.13
